TPU v7x, 256 devices: a whole 4x4x8 slice. The times are simulated.
256 devices in a mesh: brick: 32 (over z, x), scene: 8 (over y, core).
Axes of the slice: x: 4, y: 4, z: 8, core: 2. Of those that a mesh axis runs over, the one named last changes fastest.
Arguments:
- features: float32 [8, 128, 64, 512], P('scene', 'brick'), may hold values from -6 to 6
- cotangent: float32 [8, 128, 64, 512], P('scene', 'brick'), may hold values from -6 to 6
- first_kernel: float32 [27, 64, 64], replicated, may hold values from -0.15625 to 0.15625
- second_kernel: float32 [27, 64, 64], replicated, may hold values from -0.15625 to 0.15625
- counts: int32 [32], P('brick'), may hold values from 1 to 4, as said below
- neighbours: int32 [128, 26], P('brick'), may hold values from -1 to 127, as said below
Outputs:
- out_features: float32 [8, 128, 64, 512], P('scene', 'brick')
- feature_grad: float32 [8, 128, 64, 512], P('scene', 'brick')
- first_grad: float32 [27, 64, 64], replicated
- second_grad: float32 [27, 64, 64], replicated
Inputs may be any that keep to these rules, and one draw needn't show every extreme that they name: Index d of brick owns counts[d] bricks in its slots 0 to counts[d] - 1; some index owns 4. `neighbours`: entries name occupied slots; the relation is symmetric (if slot t is the neighbour of s in direction (a, b, c), s is the neighbour of t in (-a, -b, -c)); unoccupied slots have only -1. A neighbour in a direction with c = 0 is owned by the same index of brick, with c = 1 by the same or the next index, with c = -1 by the same or the previous index.
All inputs are finite; a program needn't handle non-finite values.
Results may differ from a plain program's by a relative error of at most 0.0057.
Values may be sent and summed in bfloat16 or wider, within the bound.
No kernel may reach another device: no remote copies, remote signals or barrier semaphores. Data moves between devices by JAX's collectives and lax.ppermute only.
A program may use at most 128 MiB of HBM per device.

v0:
```python
import jax
import jax.numpy as jnp
from jax import lax
from jax.sharding import PartitionSpec as P

E = 8
offsets = [(a, b, c) for a in (-1, 0, 1) for b in (-1, 0, 1) for c in (-1, 0, 1)]
directions = [item for item in offsets if item != (0, 0, 0)]


def with_halo(shard, sides, width):
    for axis, dim in sides:
        devices, length = (lax.axis_size(axis), shard.shape[dim])
        up = [(i, (i + 1) % devices) for i in range(devices - 1)]
        down = [(j, i) for i, j in up]
        last = lax.slice_in_dim(shard, length - width, length, axis=dim)
        first = lax.slice_in_dim(shard, 0, width, axis=dim)
        before = lax.ppermute(last, axis, up)
        after = lax.ppermute(first, axis, down)
        shard = jnp.concatenate([before, shard, after], axis=dim)
    return shard


def source_range(offset, edge_cells):
    if offset < 0:
        return (edge_cells - 1, edge_cells)
    if offset == 0:
        return (0, edge_cells)
    return (0, 1)


def assemble(center, sources, indices, present, edge_cells):
    pieces = {}
    pieces[0, 0, 0] = center
    for number, (a, b, c) in enumerate(directions):
        source = sources[c + 1]
        range_i = source_range(a, edge_cells)
        range_j = source_range(b, edge_cells)
        depth_range = source_range(c, edge_cells) if c == 0 else (0, 1)
        slab_part = source[
            :, :, range_i[0] : range_i[1], range_j[0] : range_j[1], depth_range[0] : depth_range[1]
        ]
        last_row = source.shape[0] - 1
        chosen_rows = jnp.clip(indices[c + 1][:, number], 0, last_row).astype(jnp.int32)
        picked = jnp.take(slab_part, chosen_rows, axis=0)
        pieces[a, b, c] = jnp.where(
            present[:, number][:, None, None, None, None], picked, jnp.zeros_like(picked)
        )
    planes = []
    for a in (-1, 0, 1):
        lines = []
        for b in (-1, 0, 1):
            lines.append(jnp.concatenate([pieces[a, b, c] for c in (-1, 0, 1)], axis=4))
        planes.append(jnp.concatenate(lines, axis=3))
    return jnp.concatenate(planes, axis=2)


def columns_of(padded):
    lead_shape = padded.shape[:3]
    stacked = []
    for number in range(27):
        a, b, c = offsets[number]
        part = padded[..., 1 + a : 1 + a + E, 1 + b : 1 + b + E, 1 + c : 1 + c + E]
        stacked.append(part.reshape(lead_shape + (E * E * E,)))
    joined = jnp.stack(stacked, axis=2)
    return joined.reshape((lead_shape[0], lead_shape[1], 27 * lead_shape[2], E * E * E))


def apply_flat(columns, weight_flat):
    return jnp.einsum("ko,nskp->nsop", weight_flat, columns, preferred_element_type=jnp.float32)


def kernel_terms(columns, errors_b):
    total = jnp.einsum("nskp,nsop->ko", columns, errors_b, preferred_element_type=jnp.float32)
    return total.reshape(27, errors_b.shape[2], errors_b.shape[2])


def slope(values):
    sig = jax.nn.sigmoid(values)
    return sig * (1.0 + values * (1.0 - sig))


def body(features, cotangent, first_kernel, second_kernel, counts, neighbours):
    scenes_here, slots_here, channels, voxels = features.shape
    device_row = lax.axis_index("brick")
    occupied = (jnp.arange(slots_here, dtype=jnp.int32) < counts[0]).astype(jnp.float32)[
        None, :, None, None
    ]
    inputs = features * occupied
    upstream = cotangent * occupied
    present = neighbours >= 0
    index_mid = neighbours - device_row * slots_here
    index_low = index_mid + slots_here
    indices = (index_low, index_mid, index_mid)
    first_b = first_kernel.astype(jnp.bfloat16)
    second_b = second_kernel.astype(jnp.bfloat16)
    first_fwd = first_b.reshape(27 * channels, channels)
    second_fwd = second_b.reshape(27 * channels, channels)
    first_back = jnp.transpose(first_b[::-1], (0, 2, 1)).reshape(27 * channels, channels)
    second_back = jnp.transpose(second_b[::-1], (0, 2, 1)).reshape(27 * channels, channels)
    cube_shape = (scenes_here, slots_here, channels, E, E, E)

    def padded_of(values):
        rounded = values.astype(jnp.bfloat16)
        cubes = rounded.reshape(cube_shape)
        extended = with_halo(rounded, (("brick", 1),), slots_here)
        below = extended[:, :slots_here].reshape(cube_shape)[..., E - 1 : E]
        above = extended[:, 2 * slots_here :].reshape(cube_shape)[..., 0:1]
        pool_low = jnp.concatenate([below, cubes[..., E - 1 : E]], axis=1)
        pool_high = jnp.concatenate([cubes[..., 0:1], above], axis=1)

        def build(centre, lower_pool, upper_pool):
            return assemble(centre, (lower_pool, centre, upper_pool), indices, present, E)

        return columns_of(jax.vmap(build)(cubes, pool_low, pool_high))

    columns_in = padded_of(inputs)
    first_pre = apply_flat(columns_in, first_fwd)
    hidden = inputs + jax.nn.silu(first_pre)
    columns_hidden = padded_of(hidden)
    second_pre = apply_flat(columns_hidden, second_fwd)
    outputs = hidden + jax.nn.silu(second_pre)
    second_err = upstream * slope(second_pre)
    hidden_grad = upstream + apply_flat(padded_of(second_err), second_back)
    second_local = kernel_terms(columns_hidden, second_err.astype(jnp.bfloat16))
    first_err = hidden_grad * slope(first_pre)
    input_grad = hidden_grad + apply_flat(padded_of(first_err), first_back)
    first_local = kernel_terms(columns_in, first_err.astype(jnp.bfloat16))
    first_total, second_total = lax.psum((first_local, second_local), ("brick", "scene"))
    total_slots = (
        lax.axis_size("brick") * lax.axis_size("scene") * scenes_here * slots_here * voxels
    )
    scale = 1.0 / jnp.sqrt(jnp.float32(total_slots))
    return (outputs, input_grad, first_total * scale, second_total * scale)


def solution(mesh):
    return jax.shard_map(
        body,
        mesh=mesh,
        in_specs=(
            P("scene", "brick", None, None),
            P("scene", "brick", None, None),
            P(),
            P(),
            P("brick"),
            P("brick", None),
        ),
        out_specs=(P("scene", "brick", None, None), P("scene", "brick", None, None), P(), P()),
        check_vma=False,
    )
```

profile of v0, /device:TPU:2, one launch (start us, length us, event | category | flops | bytes accessed | tf_op | source)
XLA Modules:
  0.0 656.1 jit_solution(11767349416236179653)
XLA Ops:
  9.2 4.2 collective-permute-start.1
  68.2 2.7 maximum_maximum_fusion.5
  72.3 2.0 maximum_maximum_fusion
  75.6 2.0 copy.455
  77.5 2.0 copy.454
  80.4 3.3 fusion.271
  88.4 2.5 fusion.263
  91.0 2.0 copy.447
  93.0 2.0 copy.446
  105.5 2.3 fusion.262
  126.8 2.2 copy-done
  129.1 3.3 fusion.254
  132.5 4.6 collective-permute-start.3
  137.1 2.1 collective-permute-start.2
  166.9 2.5 maximum_maximum_fusion.7
  170.8 2.4 maximum_maximum_fusion.1
  174.5 1.9 copy.526
  179.3 3.3 fusion.269
  182.6 2.0 copy.521
  187.3 2.5 fusion.261
  189.9 2.0 copy.518
  195.7 2.0 copy.515
  197.7 1.9 copy.514
  204.3 2.3 fusion.260
  209.2 1.9 copy.533
  226.0 3.9 multiply_convert_fusion.1
  230.0 3.8 fusion.4
  233.9 3.9 collective-permute-start.5
  237.8 2.1 collective-permute-start.4
  267.5 2.5 maximum_maximum_fusion.9
  271.4 2.2 maximum_maximum_fusion.2
  275.0 1.9 copy.597
  276.9 1.9 copy.596
  279.7 3.3 fusion.267
  285.0 2.0 copy.591
  287.9 2.5 fusion.259
  290.4 2.0 copy.589
  296.3 1.9 copy.586
  304.8 2.3 fusion.258
  344.2 3.7 copy.607
  347.9 3.4 multiply_convert_fusion
  351.4 2.9 fusion.7
  354.4 3.9 collective-permute-start.7
  358.3 4.1 collective-permute-start.6
  389.6 2.5 maximum_maximum_fusion.11
  393.5 2.0 maximum_maximum_fusion.3
  396.9 1.9 copy.668
  401.6 3.4 fusion.265
  405.1 1.9 copy.663
  407.0 1.9 copy.662
  409.9 2.6 fusion.257
  412.5 2.0 copy.660
  414.5 2.0 copy.659
  416.5 2.0 copy.658
  418.4 1.9 copy.657
  420.4 1.9 copy.656
  422.3 2.0 copy.655
  427.0 2.4 fusion.256
  431.9 1.9 copy.675
  433.9 2.0 copy.674
  448.5 3.2 fusion.11
  451.7 192.7 %all-reduce.3.cloned.1.call-done = (f32[27,64,64]{2,1,0:T(8,128)}, f32[27,64,64]{2,1,0:T(8,128)}) async-done(((f32[27,64,64]{2,1,0:T(8,128)}, f32[27,64,64]{2,1,0:T(8,128)}), (f32[27,64,64]{2,1,0:T(8,128)}, f32[27,64,64]{2,1,0:T(8,128)})) %all-reduce.3.cloned.1.call-update) | async-done | bytes 884752 | tf_op jit(solution)/shard_map/psum | solution.py:129
  644.4 2.2 broadcast_multiply_fusion.1
  646.6 2.2 broadcast_multiply_fusion
  (1379 shorter events, 282.8 us)
Async XLA Ops:
  7.2 25.6 %copy-start.98 = (f32[27,64,64]{2,1,0:T(8,128)S(1)}, f32[27,64,64]{2,1,0:T(8,128)}, u32[]{:S(2)}) copy-start(f32[27,64,64]{2,1,0:T(8,128)} %param.22) | copy-start | bytes 1327108
  7.2 25.7 %copy-start.99 = (f32[27,64,64]{2,1,0:T(8,128)S(1)}, f32[27,64,64]{2,1,0:T(8,128)}, u32[]{:S(2)}) copy-start(f32[27,64,64]{2,1,0:T(8,128)} %param.23) | copy-start | bytes 1327108
  7.2 637.2 %all-reduce.3.cloned.1.call-start = ((), (), s32[]{:S(2)}) async-start(), calls=%async_computation | async-start | bytes 3538944 | tf_op jit(solution)/shard_map/psum | solution.py:129
  9.2 40.3 %collective-permute-start.1 = (bf16[1,4,64,512]{3,2,1,0:T(8,128)(2,1)S(1)}, bf16[1,4,64,512]{3,2,1,0:T(8,128)(2,1)}, u32[]{:S(2)}, u32[]{:S(2)}) collective-permute-start(bf16[1,4,64,512]{3,2,1,0:T(8,128)(2,1)S(1)} %multiply_convert_fusion.2), channel_id=1, source_target_pairs={{8,0},{16,8},{24,16},{32,24},{40,32},{48,40},{56,48},{64,56},{72,6... | collective-permute-start | bytes 786440 | tf_op jit(solution)/shard_map/ppermute | solution.py:19
  13.3 34.3 %collective-permute-start = (bf16[1,4,64,512]{3,2,1,0:T(8,128)(2,1)S(1)}, bf16[1,4,64,512]{3,2,1,0:T(8,128)(2,1)}, u32[]{:S(2)}, u32[]{:S(2)}) collective-permute-start(bf16[1,4,64,512]{3,2,1,0:T(8,128)(2,1)S(1)} %multiply_convert_fusion.2), channel_id=1, source_target_pairs={{0,8},{8,16},{16,24},{24,32},{32,40},{40,48},{48,56},{56,64},{64,7... | collective-permute-start | bytes 786440 | tf_op jit(solution)/shard_map/ppermute | solution.py:18
  19.3 37.3 %copy-start.233 = (pred[4]{0:T(512)(128)(4,1)}, pred[4]{0:T(512)(128)(4,1)S(1)}, u32[]{:S(2)}) copy-start(pred[4]{0:T(512)(128)(4,1)S(1)} %get-tuple-element.336) | copy-start | bytes 16
  20.3 21.8 %copy-start.329 = (pred[4]{0:T(512)(128)(4,1)}, pred[4]{0:T(512)(128)(4,1)S(1)}, u32[]{:S(2)}) copy-start(pred[4]{0:T(512)(128)(4,1)S(1)} %compare_and_fusion.24) | copy-start | bytes 16
  20.9 19.8 %copy-start.253 = (pred[4]{0:T(512)(128)(4,1)}, pred[4]{0:T(512)(128)(4,1)S(1)}, u32[]{:S(2)}) copy-start(pred[4]{0:T(512)(128)(4,1)S(1)} %get-tuple-element.310) | copy-start | bytes 16
  21.4 20.1 %copy-start.249 = (pred[4]{0:T(512)(128)(4,1)}, pred[4]{0:T(512)(128)(4,1)S(1)}, u32[]{:S(2)}) copy-start(pred[4]{0:T(512)(128)(4,1)S(1)} %get-tuple-element.306) | copy-start | bytes 16
  21.9 21.1 %copy-start.153 = (pred[4]{0:T(512)(128)(4,1)}, pred[4]{0:T(512)(128)(4,1)S(1)}, u32[]{:S(2)}) copy-start(pred[4]{0:T(512)(128)(4,1)S(1)} %get-tuple-element.308) | copy-start | bytes 16
  22.5 20.4 %copy-start.157 = (pred[4]{0:T(512)(128)(4,1)}, pred[4]{0:T(512)(128)(4,1)S(1)}, u32[]{:S(2)}) copy-start(pred[4]{0:T(512)(128)(4,1)S(1)} %get-tuple-element.312) | copy-start | bytes 16
  23.7 19.1 %copy-start.165 = (pred[4]{0:T(512)(128)(4,1)}, pred[4]{0:T(512)(128)(4,1)S(1)}, u32[]{:S(2)}) copy-start(pred[4]{0:T(512)(128)(4,1)S(1)} %get-tuple-element.315) | copy-start | bytes 16
  24.2 17.2 %copy-start.257 = (pred[4]{0:T(512)(128)(4,1)}, pred[4]{0:T(512)(128)(4,1)S(1)}, u32[]{:S(2)}) copy-start(pred[4]{0:T(512)(128)(4,1)S(1)} %get-tuple-element.317) | copy-start | bytes 16
  24.8 22.7 %copy-start.161 = (pred[4]{0:T(512)(128)(4,1)}, pred[4]{0:T(512)(128)(4,1)S(1)}, u32[]{:S(2)}) copy-start(pred[4]{0:T(512)(128)(4,1)S(1)} %get-tuple-element.319) | copy-start | bytes 16
  25.6 16.6 %copy-start.177 = (pred[4]{0:T(512)(128)(4,1)}, pred[4]{0:T(512)(128)(4,1)S(1)}, u32[]{:S(2)}) copy-start(pred[4]{0:T(512)(128)(4,1)S(1)} %get-tuple-element.62) | copy-start | bytes 16
  25.6 21.9 %copy-start.121 = (pred[4]{0:T(512)(128)(4,1)}, pred[4]{0:T(512)(128)(4,1)S(1)}, u32[]{:S(2)}) copy-start(pred[4]{0:T(512)(128)(4,1)S(1)} %get-tuple-element.59) | copy-start | bytes 16
  25.6 30.1 %copy-start.173 = (pred[4]{0:T(512)(128)(4,1)}, pred[4]{0:T(512)(128)(4,1)S(1)}, u32[]{:S(2)}) copy-start(pred[4]{0:T(512)(128)(4,1)S(1)} %get-tuple-element.60) | copy-start | bytes 16
  26.6 14.1 %copy-start.213 = (pred[4]{0:T(512)(128)(4,1)}, pred[4]{0:T(512)(128)(4,1)S(1)}, u32[]{:S(2)}) copy-start(pred[4]{0:T(512)(128)(4,1)S(1)} %get-tuple-element.45) | copy-start | bytes 16
  26.6 14.8 %copy-start.209 = (pred[4]{0:T(512)(128)(4,1)}, pred[4]{0:T(512)(128)(4,1)S(1)}, u32[]{:S(2)}) copy-start(pred[4]{0:T(512)(128)(4,1)S(1)} %get-tuple-element.55) | copy-start | bytes 16
  26.6 14.9 %copy-start.205 = (pred[4]{0:T(512)(128)(4,1)}, pred[4]{0:T(512)(128)(4,1)S(1)}, u32[]{:S(2)}) copy-start(pred[4]{0:T(512)(128)(4,1)S(1)} %get-tuple-element.39) | copy-start | bytes 16
  26.6 16.3 %copy-start.141 = (pred[4]{0:T(512)(128)(4,1)}, pred[4]{0:T(512)(128)(4,1)S(1)}, u32[]{:S(2)}) copy-start(pred[4]{0:T(512)(128)(4,1)S(1)} %get-tuple-element.52) | copy-start | bytes 16
  26.6 16.4 %copy-start.137 = (pred[4]{0:T(512)(128)(4,1)}, pred[4]{0:T(512)(128)(4,1)S(1)}, u32[]{:S(2)}) copy-start(pred[4]{0:T(512)(128)(4,1)S(1)} %get-tuple-element.47) | copy-start | bytes 16
  26.6 16.5 %copy-start.133 = (pred[4]{0:T(512)(128)(4,1)}, pred[4]{0:T(512)(128)(4,1)S(1)}, u32[]{:S(2)}) copy-start(pred[4]{0:T(512)(128)(4,1)S(1)} %get-tuple-element.42) | copy-start | bytes 16
  26.6 28.3 %copy-start.201 = (pred[4]{0:T(512)(128)(4,1)}, pred[4]{0:T(512)(128)(4,1)S(1)}, u32[]{:S(2)}) copy-start(pred[4]{0:T(512)(128)(4,1)S(1)} %get-tuple-element.43) | copy-start | bytes 16
  26.6 30.0 %copy-start.197 = (pred[4]{0:T(512)(128)(4,1)}, pred[4]{0:T(512)(128)(4,1)S(1)}, u32[]{:S(2)}) copy-start(pred[4]{0:T(512)(128)(4,1)S(1)} %get-tuple-element.53) | copy-start | bytes 16
  27.9 19.0 %copy-start.321 = (s32[1024]{0:T(1024)}, s32[1024]{0:T(1024)S(1)}, u32[]{:S(2)}) copy-start(s32[1024]{0:T(1024)S(1)} %pad_clamp_fusion.21) | copy-start | bytes 12292
  43.0 28.0 %copy-start.33 = (bf16[1,4,64,8,1,8]{2,5,4,3,1,0:T(8,128)(2,1)}, bf16[1,4,64,8,1,8]{2,5,4,3,1,0:T(8,128)(2,1)S(1)}, u32[]{:S(2)}) copy-start(bf16[1,4,64,8,1,8]{2,5,4,3,1,0:T(8,128)(2,1)S(1)} %fusion.41) | copy-start | bytes 98308
  49.1 14.0 %copy-start.169 = (pred[4]{0:T(512)(128)(4,1)S(1)}, pred[4]{0:T(512)(128)(4,1)}, u32[]{:S(2)}) copy-start(pred[4]{0:T(512)(128)(4,1)} %get-tuple-element.58) | copy-start | bytes 16
  49.3 14.7 %copy-start.185 = (pred[4]{0:T(512)(128)(4,1)S(1)}, pred[4]{0:T(512)(128)(4,1)}, u32[]{:S(2)}) copy-start(pred[4]{0:T(512)(128)(4,1)} %get-tuple-element.51) | copy-start | bytes 16
  49.3 14.7 %copy-start.221 = (pred[4]{0:T(512)(128)(4,1)S(1)}, pred[4]{0:T(512)(128)(4,1)}, u32[]{:S(2)}) copy-start(pred[4]{0:T(512)(128)(4,1)} %get-tuple-element.314) | copy-start | bytes 16
  49.3 15.4 %copy-start.181 = (pred[4]{0:T(512)(128)(4,1)S(1)}, pred[4]{0:T(512)(128)(4,1)}, u32[]{:S(2)}) copy-start(pred[4]{0:T(512)(128)(4,1)} %get-tuple-element.46) | copy-start | bytes 16
  49.3 15.4 %copy-start.217 = (pred[4]{0:T(512)(128)(4,1)S(1)}, pred[4]{0:T(512)(128)(4,1)}, u32[]{:S(2)}) copy-start(pred[4]{0:T(512)(128)(4,1)} %get-tuple-element.311) | copy-start | bytes 16
  50.8 14.8 %copy-start.125 = (pred[4]{0:T(512)(128)(4,1)S(1)}, pred[4]{0:T(512)(128)(4,1)}, u32[]{:S(2)}) copy-start(pred[4]{0:T(512)(128)(4,1)} %get-tuple-element.49) | copy-start | bytes 16
  50.8 14.8 %copy-start.145 = (pred[4]{0:T(512)(128)(4,1)S(1)}, pred[4]{0:T(512)(128)(4,1)}, u32[]{:S(2)}) copy-start(pred[4]{0:T(512)(128)(4,1)} %get-tuple-element.313) | copy-start | bytes 16
  132.5 16.5 %collective-permute-start.3 = (bf16[1,4,64,512]{3,2,1,0:T(8,128)(2,1)}, bf16[1,4,64,512]{3,2,1,0:T(8,128)(2,1)S(1)}, u32[]{:S(2)}, u32[]{:S(2)}) collective-permute-start(bf16[1,4,64,512]{3,2,1,0:T(8,128)(2,1)} %get-tuple-element.285), channel_id=1, source_target_pairs={{8,0},{16,8},{24,16},{32,24},{40,32},{48,40},{56,48},{64,56},{72,6... | collective-permute-start | bytes 786440 | tf_op jit(solution)/shard_map/ppermute | solution.py:19
  137.1 11.0 %collective-permute-start.2 = (bf16[1,4,64,512]{3,2,1,0:T(8,128)(2,1)}, bf16[1,4,64,512]{3,2,1,0:T(8,128)(2,1)S(1)}, u32[]{:S(2)}, u32[]{:S(2)}) collective-permute-start(bf16[1,4,64,512]{3,2,1,0:T(8,128)(2,1)} %get-tuple-element.285), channel_id=1, source_target_pairs={{0,8},{8,16},{16,24},{24,32},{32,40},{40,48},{48,56},{56,64},{64,7... | collective-permute-start | bytes 786440 | tf_op jit(solution)/shard_map/ppermute | solution.py:18
  145.4 24.2 %copy-start.34 = (bf16[1,4,64,8,1,8]{2,5,4,3,1,0:T(8,128)(2,1)}, bf16[1,4,64,8,1,8]{2,5,4,3,1,0:T(8,128)(2,1)S(1)}, u32[]{:S(2)}) copy-start(bf16[1,4,64,8,1,8]{2,5,4,3,1,0:T(8,128)(2,1)S(1)} %fusion.35) | copy-start | bytes 98308
  149.3 14.1 %copy-start.186 = (pred[4]{0:T(512)(128)(4,1)S(1)}, pred[4]{0:T(512)(128)(4,1)}, u32[]{:S(2)}) copy-start(pred[4]{0:T(512)(128)(4,1)} %get-tuple-element.51) | copy-start | bytes 16
  149.3 14.1 %copy-start.222 = (pred[4]{0:T(512)(128)(4,1)S(1)}, pred[4]{0:T(512)(128)(4,1)}, u32[]{:S(2)}) copy-start(pred[4]{0:T(512)(128)(4,1)} %get-tuple-element.314) | copy-start | bytes 16
  149.4 14.8 %copy-start.182 = (pred[4]{0:T(512)(128)(4,1)S(1)}, pred[4]{0:T(512)(128)(4,1)}, u32[]{:S(2)}) copy-start(pred[4]{0:T(512)(128)(4,1)} %get-tuple-element.46) | copy-start | bytes 16
  149.4 14.8 %copy-start.218 = (pred[4]{0:T(512)(128)(4,1)S(1)}, pred[4]{0:T(512)(128)(4,1)}, u32[]{:S(2)}) copy-start(pred[4]{0:T(512)(128)(4,1)} %get-tuple-element.311) | copy-start | bytes 16
  233.9 15.8 %collective-permute-start.5 = (bf16[1,4,64,512]{3,2,1,0:T(8,128)(2,1)}, bf16[1,4,64,512]{3,2,1,0:T(8,128)(2,1)S(1)}, u32[]{:S(2)}, u32[]{:S(2)}) collective-permute-start(bf16[1,4,64,512]{3,2,1,0:T(8,128)(2,1)} %get-tuple-element.171), channel_id=1, source_target_pairs={{8,0},{16,8},{24,16},{32,24},{40,32},{48,40},{56,48},{64,56},{72,6... | collective-permute-start | bytes 786440 | tf_op jit(solution)/shard_map/ppermute | solution.py:19
  237.8 11.0 %collective-permute-start.4 = (bf16[1,4,64,512]{3,2,1,0:T(8,128)(2,1)}, bf16[1,4,64,512]{3,2,1,0:T(8,128)(2,1)S(1)}, u32[]{:S(2)}, u32[]{:S(2)}) collective-permute-start(bf16[1,4,64,512]{3,2,1,0:T(8,128)(2,1)} %get-tuple-element.171), channel_id=1, source_target_pairs={{0,8},{8,16},{16,24},{24,32},{32,40},{40,48},{48,56},{56,64},{64,7... | collective-permute-start | bytes 786440 | tf_op jit(solution)/shard_map/ppermute | solution.py:18
  246.0 24.1 %copy-start.35 = (bf16[1,4,64,8,1,8]{2,5,4,3,1,0:T(8,128)(2,1)}, bf16[1,4,64,8,1,8]{2,5,4,3,1,0:T(8,128)(2,1)S(1)}, u32[]{:S(2)}) copy-start(bf16[1,4,64,8,1,8]{2,5,4,3,1,0:T(8,128)(2,1)S(1)} %fusion.29) | copy-start | bytes 98308
  250.0 14.1 %copy-start.187 = (pred[4]{0:T(512)(128)(4,1)S(1)}, pred[4]{0:T(512)(128)(4,1)}, u32[]{:S(2)}) copy-start(pred[4]{0:T(512)(128)(4,1)} %get-tuple-element.51) | copy-start | bytes 16
  250.0 14.1 %copy-start.223 = (pred[4]{0:T(512)(128)(4,1)S(1)}, pred[4]{0:T(512)(128)(4,1)}, u32[]{:S(2)}) copy-start(pred[4]{0:T(512)(128)(4,1)} %get-tuple-element.314) | copy-start | bytes 16
  250.1 14.8 %copy-start.183 = (pred[4]{0:T(512)(128)(4,1)S(1)}, pred[4]{0:T(512)(128)(4,1)}, u32[]{:S(2)}) copy-start(pred[4]{0:T(512)(128)(4,1)} %get-tuple-element.46) | copy-start | bytes 16
  250.1 14.8 %copy-start.219 = (pred[4]{0:T(512)(128)(4,1)S(1)}, pred[4]{0:T(512)(128)(4,1)}, u32[]{:S(2)}) copy-start(pred[4]{0:T(512)(128)(4,1)} %get-tuple-element.311) | copy-start | bytes 16
  315.8 14.4 %copy-start.66 = (bf16[1,4,1,64,512]{4,3,1,2,0:T(8,128)(2,1)S(1)}, bf16[1,4,1,64,512]{4,3,1,2,0:T(8,128)(2,1)}, u32[]{:S(2)}) copy-start(bf16[1,4,1,64,512]{4,3,1,2,0:T(8,128)(2,1)} %copy.590) | copy-start | bytes 786436
  315.8 15.1 %copy-start.62 = (bf16[1,4,1,64,512]{4,3,1,2,0:T(8,128)(2,1)S(1)}, bf16[1,4,1,64,512]{4,3,1,2,0:T(8,128)(2,1)}, u32[]{:S(2)}) copy-start(bf16[1,4,1,64,512]{4,3,1,2,0:T(8,128)(2,1)} %copy.591) | copy-start | bytes 786436
  316.7 14.9 %copy-start.58 = (bf16[1,4,1,64,512]{4,3,1,2,0:T(8,128)(2,1)S(1)}, bf16[1,4,1,64,512]{4,3,1,2,0:T(8,128)(2,1)}, u32[]{:S(2)}) copy-start(bf16[1,4,1,64,512]{4,3,1,2,0:T(8,128)(2,1)} %copy.592) | copy-start | bytes 786436
  351.4 14.4 %copy-start.208 = (pred[4]{0:T(512)(128)(4,1)S(1)}, pred[4]{0:T(512)(128)(4,1)}, u32[]{:S(2)}) copy-start(pred[4]{0:T(512)(128)(4,1)} %copy-done.205) | copy-start | bytes 16
  351.4 14.4 %copy-start.252 = (pred[4]{0:T(512)(128)(4,1)S(1)}, pred[4]{0:T(512)(128)(4,1)}, u32[]{:S(2)}) copy-start(pred[4]{0:T(512)(128)(4,1)} %copy-done.249) | copy-start | bytes 16
  354.3 14.6 %copy-start.136 = (pred[4]{0:T(512)(128)(4,1)S(1)}, pred[4]{0:T(512)(128)(4,1)}, u32[]{:S(2)}) copy-start(pred[4]{0:T(512)(128)(4,1)} %copy-done.133) | copy-start | bytes 16
  354.3 14.6 %copy-start.156 = (pred[4]{0:T(512)(128)(4,1)S(1)}, pred[4]{0:T(512)(128)(4,1)}, u32[]{:S(2)}) copy-start(pred[4]{0:T(512)(128)(4,1)} %copy-done.153) | copy-start | bytes 16
  354.3 14.7 %copy-start.180 = (pred[4]{0:T(512)(128)(4,1)S(1)}, pred[4]{0:T(512)(128)(4,1)}, u32[]{:S(2)}) copy-start(pred[4]{0:T(512)(128)(4,1)} %copy-done.177) | copy-start | bytes 16
  354.3 14.7 %copy-start.332 = (pred[4]{0:T(512)(128)(4,1)S(1)}, pred[4]{0:T(512)(128)(4,1)}, u32[]{:S(2)}) copy-start(pred[4]{0:T(512)(128)(4,1)} %copy-done.329) | copy-start | bytes 16
  354.4 17.4 %collective-permute-start.7 = (bf16[1,4,64,512]{3,2,1,0:T(8,128)(2,1)S(1)}, bf16[1,4,64,512]{3,2,1,0:T(8,128)(2,1)S(1)}, u32[]{:S(2)}, u32[]{:S(2)}) collective-permute-start(bf16[1,4,64,512]{3,2,1,0:T(8,128)(2,1)S(1)} %get-tuple-element.287), channel_id=1, source_target_pairs={{8,0},{16,8},{24,16},{32,24},{40,32},{48,40},{56,48},{64,56},{72,6... | collective-permute-start | bytes 786440 | tf_op jit(solution)/shard_map/ppermute | solution.py:19
  358.3 12.6 %collective-permute-start.6 = (bf16[1,4,64,512]{3,2,1,0:T(8,128)(2,1)S(1)}, bf16[1,4,64,512]{3,2,1,0:T(8,128)(2,1)S(1)}, u32[]{:S(2)}, u32[]{:S(2)}) collective-permute-start(bf16[1,4,64,512]{3,2,1,0:T(8,128)(2,1)S(1)} %get-tuple-element.287), channel_id=1, source_target_pairs={{0,8},{8,16},{16,24},{24,32},{32,40},{40,48},{48,56},{56,64},{64,7... | collective-permute-start | bytes 786440 | tf_op jit(solution)/shard_map/ppermute | solution.py:18
  368.2 24.0 %copy-start.32 = (bf16[1,4,64,8,1,8]{2,5,4,3,1,0:T(8,128)(2,1)}, bf16[1,4,64,8,1,8]{2,5,4,3,1,0:T(8,128)(2,1)S(1)}, u32[]{:S(2)}) copy-start(bf16[1,4,64,8,1,8]{2,5,4,3,1,0:T(8,128)(2,1)S(1)} %fusion.23) | copy-start | bytes 98308
  372.0 14.1 %copy-start.188 = (pred[4]{0:T(512)(128)(4,1)S(1)}, pred[4]{0:T(512)(128)(4,1)}, u32[]{:S(2)}) copy-start(pred[4]{0:T(512)(128)(4,1)} %get-tuple-element.51) | copy-start | bytes 16
  372.0 14.1 %copy-start.224 = (pred[4]{0:T(512)(128)(4,1)S(1)}, pred[4]{0:T(512)(128)(4,1)}, u32[]{:S(2)}) copy-start(pred[4]{0:T(512)(128)(4,1)} %get-tuple-element.314) | copy-start | bytes 16
  372.1 14.8 %copy-start.184 = (pred[4]{0:T(512)(128)(4,1)S(1)}, pred[4]{0:T(512)(128)(4,1)}, u32[]{:S(2)}) copy-start(pred[4]{0:T(512)(128)(4,1)} %get-tuple-element.46) | copy-start | bytes 16
  372.1 14.8 %copy-start.220 = (pred[4]{0:T(512)(128)(4,1)S(1)}, pred[4]{0:T(512)(128)(4,1)}, u32[]{:S(2)}) copy-start(pred[4]{0:T(512)(128)(4,1)} %get-tuple-element.311) | copy-start | bytes 16
  (288 other events, 2396.4 us)
Sparse Core Ops, SparseCore 0:
  370.8 273.5 all-reduce.2
where the time goes:
time: 667 us; the launch traced here: 656 us
  local copies, waits for them, and re-layouts  330 us (49%)
  waiting for transfers between devices  193 us (29%)
  other arithmetic  63.3 us (9%)
  starting transfers between devices  26.9 us (4%)
  between operations  22.1 us (3%)
  matrix products  20.5 us (3%)
    psum x1, waiting for transfers between devices, body(): lax.psum((first_local, second_local), ('brick', 'scene'))  193 us
    another operation x112, local copies, waits for them, and re-layouts, columns_of(): joined = jnp.stack(stacked, axis=2)  148 us
    gather x104, local copies, waits for them, and re-layouts, assemble(): picked = jnp.take(slab_part, chosen_rows, axis=0)  70.4 us
    unnamed x805, local copies, waits for them, and re-layouts  57.1 us
    slice x16, local copies, waits for them, and re-layouts, columns_of(): part = padded[..., 1 + a:1 + a + E, 1 + b:1 + b + E, 1 + c:1 + c + E]  38.4 us
    ppermute x4, starting transfers between devices, with_halo(): after = lax.ppermute(first, axis, down)  16.6 us
    dot_general x4, matrix products, apply_flat(): jnp.einsum('ko,nskp->nsop', weight_flat, columns, preferred_element_type=...  13.8 us
  transfers between devices with their start and end apart: 9, of which 1 were waited for; matrix products, arithmetic and copies ran while one was open for 21% of the time, Pallas kernels for 0%

commit v1 on v0

--- a/solution.py
+++ b/solution.py
@@ -126,7 +126,7 @@
     first_err = hidden_grad * slope(first_pre)
     input_grad = hidden_grad + apply_flat(padded_of(first_err), first_back)
     first_local = kernel_terms(columns_in, first_err.astype(jnp.bfloat16))
-    first_total, second_total = lax.psum((first_local, second_local), ("brick", "scene"))
+    first_total, second_total = lax.psum(lax.psum((first_local, second_local), "scene"), "brick")
     total_slots = (
         lax.axis_size("brick") * lax.axis_size("scene") * scenes_here * slots_here * voxels
     )

time: 667 us -> 650 us (0.975)
  waiting for transfers between devices: 193 us -> 153 us
  local copies, waits for them, and re-layouts: 330 us -> 353 us
    psum x1 -> x2, waiting for transfers between devices: 193 us -> 153 us  [the longest x1 153 us: body(): lax.psum(lax.psum((first_local, second_local), 'scene'), 'brick')]
    unnamed x805 -> x803, local copies, waits for them, and re-layouts: 57.1 us -> 76.7 us
  transfers between devices with their start and end apart: 9 -> 10, of which waited for: 1 -> 1; matrix products, arithmetic and copies ran while one was open for 21% -> 25% of each run, Pallas kernels for 0% -> 0%
where the time goes in v1:
time: 650 us; the launch traced here: 637 us
  local copies, waits for them, and re-layouts  353 us (54%)
  waiting for transfers between devices  153 us (24%)
  other arithmetic  63.2 us (10%)
  starting transfers between devices  27 us (4%)
  between operations  21.8 us (3%)
  matrix products  19.5 us (3%)
    psum x1, waiting for transfers between devices, body(): lax.psum(lax.psum((first_local, second_local), 'scene'), 'brick')  153 us
    another operation x112, local copies, waits for them, and re-layouts, columns_of(): joined = jnp.stack(stacked, axis=2)  152 us
    unnamed x803, local copies, waits for them, and re-layouts  76.7 us
    gather x104, local copies, waits for them, and re-layouts, assemble(): picked = jnp.take(slab_part, chosen_rows, axis=0)  70.4 us
    slice x16, local copies, waits for them, and re-layouts, columns_of(): part = padded[..., 1 + a:1 + a + E, 1 + b:1 + b + E, 1 + c:1 + c + E]  37.7 us
    ppermute x4, starting transfers between devices, with_halo(): after = lax.ppermute(first, axis, down)  16.6 us
  transfers between devices with their start and end apart: 10, of which 1 were waited for; matrix products, arithmetic and copies ran while one was open for 25% of the time, Pallas kernels for 0%

profile of v1, /device:TPU:2, one launch (start us, length us, event | category | flops | bytes accessed | tf_op | source)
XLA Modules:
  0.0 637.1 jit_solution(12205020935142175207)
XLA Ops:
  9.2 4.2 collective-permute-start.1
  68.2 2.7 maximum_maximum_fusion.5
  72.2 2.0 maximum_maximum_fusion
  75.5 2.0 copy.455
  77.5 2.0 copy.454
  80.3 3.3 fusion.271
  88.4 2.5 fusion.263
  91.0 2.0 copy.447
  93.0 1.9 copy.446
  105.4 2.3 fusion.262
  110.3 1.9 copy.462
  126.8 2.2 copy-done
  129.1 3.3 fusion.254
  132.5 4.6 collective-permute-start.3
  137.1 2.1 collective-permute-start.2
  166.9 2.5 maximum_maximum_fusion.7
  170.8 2.4 maximum_maximum_fusion.1
  179.2 3.2 fusion.269
  182.4 2.0 copy.521
  187.1 2.5 fusion.261
  189.7 2.0 copy.518
  191.7 1.9 copy.517
  193.6 1.9 copy.516
  195.5 1.9 copy.515
  197.5 1.9 copy.514
  204.1 2.3 fusion.260
  208.9 1.9 copy.533
  210.9 1.9 copy.532
  225.8 3.9 multiply_convert_fusion.1
  229.7 3.8 fusion.4
  233.6 3.9 collective-permute-start.5
  237.6 2.1 collective-permute-start.4
  267.3 2.5 maximum_maximum_fusion.9
  271.1 2.2 maximum_maximum_fusion.2
  274.7 1.9 copy.597
  276.6 2.0 copy.596
  279.5 3.2 fusion.267
  284.6 1.9 copy.591
  287.4 2.5 fusion.259
  289.9 2.0 copy.589
  293.9 1.9 copy.587
  297.7 1.9 copy.585
  304.3 2.3 fusion.258
  343.7 3.7 copy.607
  347.4 3.4 multiply_convert_fusion
  350.9 2.9 fusion.7
  353.8 3.9 collective-permute-start.7
  357.7 4.1 collective-permute-start.6
  389.1 2.5 maximum_maximum_fusion.11
  392.9 2.0 maximum_maximum_fusion.3
  398.2 2.0 copy.667
  401.1 3.4 fusion.265
  404.4 2.0 copy.663
  409.2 2.5 fusion.257
  411.7 2.0 copy.660
  417.6 1.9 copy.657
  426.1 2.3 fusion.256
  429.7 2.0 copy.673
  433.6 2.0 copy.671
  466.6 3.6 copy.678
  470.2 2.1 fusion.11
  472.4 153.1 %all-reduce.5.cloned.1.call-done = (f32[27,64,64]{2,1,0:T(8,128)}, f32[27,64,64]{2,1,0:T(8,128)}) async-done(((f32[27,64,64]{2,1,0:T(8,128)}, f32[27,64,64]{2,1,0:T(8,128)}), (f32[27,64,64]{2,1,0:T(8,128)}, f32[27,64,64]{2,1,0:T(8,128)})) %all-reduce.5.cloned.1.call-update) | async-done | bytes 884752 | tf_op jit(solution)/shard_map/psum | solution.py:129
  625.5 2.2 broadcast_multiply_fusion.1
  627.7 2.2 broadcast_multiply_fusion
  (1380 shorter events, 303.8 us)
Async XLA Ops:
  7.2 25.5 %copy-start.97 = (f32[27,64,64]{2,1,0:T(8,128)S(1)}, f32[27,64,64]{2,1,0:T(8,128)}, u32[]{:S(2)}) copy-start(f32[27,64,64]{2,1,0:T(8,128)} %param.22) | copy-start | bytes 1327108
  7.2 25.6 %copy-start.98 = (f32[27,64,64]{2,1,0:T(8,128)S(1)}, f32[27,64,64]{2,1,0:T(8,128)}, u32[]{:S(2)}) copy-start(f32[27,64,64]{2,1,0:T(8,128)} %param.23) | copy-start | bytes 1327108
  7.2 455.9 %all-reduce.7.cloned.1.call-start = ((), (), s32[]{:S(2)}) async-start(), calls=%async_computation.1 | async-start | bytes 3538944 | tf_op jit(solution)/shard_map/psum | solution.py:129
  9.2 40.2 %collective-permute-start.1 = (bf16[1,4,64,512]{3,2,1,0:T(8,128)(2,1)S(1)}, bf16[1,4,64,512]{3,2,1,0:T(8,128)(2,1)}, u32[]{:S(2)}, u32[]{:S(2)}) collective-permute-start(bf16[1,4,64,512]{3,2,1,0:T(8,128)(2,1)S(1)} %multiply_convert_fusion.2), channel_id=1, source_target_pairs={{8,0},{16,8},{24,16},{32,24},{40,32},{48,40},{56,48},{64,56},{72,6... | collective-permute-start | bytes 786440 | tf_op jit(solution)/shard_map/ppermute | solution.py:19
  13.3 34.2 %collective-permute-start = (bf16[1,4,64,512]{3,2,1,0:T(8,128)(2,1)S(1)}, bf16[1,4,64,512]{3,2,1,0:T(8,128)(2,1)}, u32[]{:S(2)}, u32[]{:S(2)}) collective-permute-start(bf16[1,4,64,512]{3,2,1,0:T(8,128)(2,1)S(1)} %multiply_convert_fusion.2), channel_id=1, source_target_pairs={{0,8},{8,16},{16,24},{24,32},{32,40},{40,48},{48,56},{56,64},{64,7... | collective-permute-start | bytes 786440 | tf_op jit(solution)/shard_map/ppermute | solution.py:18
  19.3 37.2 %copy-start.232 = (pred[4]{0:T(512)(128)(4,1)}, pred[4]{0:T(512)(128)(4,1)S(1)}, u32[]{:S(2)}) copy-start(pred[4]{0:T(512)(128)(4,1)S(1)} %get-tuple-element.338) | copy-start | bytes 16
  20.3 21.7 %copy-start.328 = (pred[4]{0:T(512)(128)(4,1)}, pred[4]{0:T(512)(128)(4,1)S(1)}, u32[]{:S(2)}) copy-start(pred[4]{0:T(512)(128)(4,1)S(1)} %compare_and_fusion.24) | copy-start | bytes 16
  20.9 19.7 %copy-start.252 = (pred[4]{0:T(512)(128)(4,1)}, pred[4]{0:T(512)(128)(4,1)S(1)}, u32[]{:S(2)}) copy-start(pred[4]{0:T(512)(128)(4,1)S(1)} %get-tuple-element.312) | copy-start | bytes 16
  21.4 20.0 %copy-start.248 = (pred[4]{0:T(512)(128)(4,1)}, pred[4]{0:T(512)(128)(4,1)S(1)}, u32[]{:S(2)}) copy-start(pred[4]{0:T(512)(128)(4,1)S(1)} %get-tuple-element.308) | copy-start | bytes 16
  21.9 21.1 %copy-start.152 = (pred[4]{0:T(512)(128)(4,1)}, pred[4]{0:T(512)(128)(4,1)S(1)}, u32[]{:S(2)}) copy-start(pred[4]{0:T(512)(128)(4,1)S(1)} %get-tuple-element.310) | copy-start | bytes 16
  22.4 20.4 %copy-start.160 = (pred[4]{0:T(512)(128)(4,1)}, pred[4]{0:T(512)(128)(4,1)S(1)}, u32[]{:S(2)}) copy-start(pred[4]{0:T(512)(128)(4,1)S(1)} %get-tuple-element.314) | copy-start | bytes 16
  23.6 19.1 %copy-start.164 = (pred[4]{0:T(512)(128)(4,1)}, pred[4]{0:T(512)(128)(4,1)S(1)}, u32[]{:S(2)}) copy-start(pred[4]{0:T(512)(128)(4,1)S(1)} %get-tuple-element.317) | copy-start | bytes 16
  24.1 17.1 %copy-start.256 = (pred[4]{0:T(512)(128)(4,1)}, pred[4]{0:T(512)(128)(4,1)S(1)}, u32[]{:S(2)}) copy-start(pred[4]{0:T(512)(128)(4,1)S(1)} %get-tuple-element.319) | copy-start | bytes 16
  24.7 22.7 %copy-start.156 = (pred[4]{0:T(512)(128)(4,1)}, pred[4]{0:T(512)(128)(4,1)S(1)}, u32[]{:S(2)}) copy-start(pred[4]{0:T(512)(128)(4,1)S(1)} %get-tuple-element.321) | copy-start | bytes 16
  25.5 16.6 %copy-start.176 = (pred[4]{0:T(512)(128)(4,1)}, pred[4]{0:T(512)(128)(4,1)S(1)}, u32[]{:S(2)}) copy-start(pred[4]{0:T(512)(128)(4,1)S(1)} %get-tuple-element.62) | copy-start | bytes 16
  25.5 21.9 %copy-start.120 = (pred[4]{0:T(512)(128)(4,1)}, pred[4]{0:T(512)(128)(4,1)S(1)}, u32[]{:S(2)}) copy-start(pred[4]{0:T(512)(128)(4,1)S(1)} %get-tuple-element.59) | copy-start | bytes 16
  25.5 30.1 %copy-start.172 = (pred[4]{0:T(512)(128)(4,1)}, pred[4]{0:T(512)(128)(4,1)S(1)}, u32[]{:S(2)}) copy-start(pred[4]{0:T(512)(128)(4,1)S(1)} %get-tuple-element.60) | copy-start | bytes 16
  26.5 14.1 %copy-start.212 = (pred[4]{0:T(512)(128)(4,1)}, pred[4]{0:T(512)(128)(4,1)S(1)}, u32[]{:S(2)}) copy-start(pred[4]{0:T(512)(128)(4,1)S(1)} %get-tuple-element.45) | copy-start | bytes 16
  26.5 14.8 %copy-start.208 = (pred[4]{0:T(512)(128)(4,1)}, pred[4]{0:T(512)(128)(4,1)S(1)}, u32[]{:S(2)}) copy-start(pred[4]{0:T(512)(128)(4,1)S(1)} %get-tuple-element.55) | copy-start | bytes 16
  26.5 14.9 %copy-start.204 = (pred[4]{0:T(512)(128)(4,1)}, pred[4]{0:T(512)(128)(4,1)S(1)}, u32[]{:S(2)}) copy-start(pred[4]{0:T(512)(128)(4,1)S(1)} %get-tuple-element.39) | copy-start | bytes 16
  26.5 16.2 %copy-start.140 = (pred[4]{0:T(512)(128)(4,1)}, pred[4]{0:T(512)(128)(4,1)S(1)}, u32[]{:S(2)}) copy-start(pred[4]{0:T(512)(128)(4,1)S(1)} %get-tuple-element.52) | copy-start | bytes 16
  26.5 16.3 %copy-start.136 = (pred[4]{0:T(512)(128)(4,1)}, pred[4]{0:T(512)(128)(4,1)S(1)}, u32[]{:S(2)}) copy-start(pred[4]{0:T(512)(128)(4,1)S(1)} %get-tuple-element.47) | copy-start | bytes 16
  26.5 16.5 %copy-start.132 = (pred[4]{0:T(512)(128)(4,1)}, pred[4]{0:T(512)(128)(4,1)S(1)}, u32[]{:S(2)}) copy-start(pred[4]{0:T(512)(128)(4,1)S(1)} %get-tuple-element.42) | copy-start | bytes 16
  26.5 28.3 %copy-start.200 = (pred[4]{0:T(512)(128)(4,1)}, pred[4]{0:T(512)(128)(4,1)S(1)}, u32[]{:S(2)}) copy-start(pred[4]{0:T(512)(128)(4,1)S(1)} %get-tuple-element.43) | copy-start | bytes 16
  26.5 30.0 %copy-start.196 = (pred[4]{0:T(512)(128)(4,1)}, pred[4]{0:T(512)(128)(4,1)S(1)}, u32[]{:S(2)}) copy-start(pred[4]{0:T(512)(128)(4,1)S(1)} %get-tuple-element.53) | copy-start | bytes 16
  27.8 19.0 %copy-start.320 = (s32[1024]{0:T(1024)}, s32[1024]{0:T(1024)S(1)}, u32[]{:S(2)}) copy-start(s32[1024]{0:T(1024)S(1)} %pad_clamp_fusion.21) | copy-start | bytes 12292
  42.9 28.1 %copy-start.34 = (bf16[1,4,64,8,1,8]{2,5,4,3,1,0:T(8,128)(2,1)}, bf16[1,4,64,8,1,8]{2,5,4,3,1,0:T(8,128)(2,1)S(1)}, u32[]{:S(2)}) copy-start(bf16[1,4,64,8,1,8]{2,5,4,3,1,0:T(8,128)(2,1)S(1)} %fusion.41) | copy-start | bytes 98308
  49.2 14.7 %copy-start.184 = (pred[4]{0:T(512)(128)(4,1)S(1)}, pred[4]{0:T(512)(128)(4,1)}, u32[]{:S(2)}) copy-start(pred[4]{0:T(512)(128)(4,1)} %get-tuple-element.51) | copy-start | bytes 16
  49.2 14.7 %copy-start.220 = (pred[4]{0:T(512)(128)(4,1)S(1)}, pred[4]{0:T(512)(128)(4,1)}, u32[]{:S(2)}) copy-start(pred[4]{0:T(512)(128)(4,1)} %get-tuple-element.316) | copy-start | bytes 16
  49.2 15.4 %copy-start.180 = (pred[4]{0:T(512)(128)(4,1)S(1)}, pred[4]{0:T(512)(128)(4,1)}, u32[]{:S(2)}) copy-start(pred[4]{0:T(512)(128)(4,1)} %get-tuple-element.46) | copy-start | bytes 16
  49.2 15.4 %copy-start.216 = (pred[4]{0:T(512)(128)(4,1)S(1)}, pred[4]{0:T(512)(128)(4,1)}, u32[]{:S(2)}) copy-start(pred[4]{0:T(512)(128)(4,1)} %get-tuple-element.313) | copy-start | bytes 16
  50.7 14.8 %copy-start.124 = (pred[4]{0:T(512)(128)(4,1)S(1)}, pred[4]{0:T(512)(128)(4,1)}, u32[]{:S(2)}) copy-start(pred[4]{0:T(512)(128)(4,1)} %get-tuple-element.49) | copy-start | bytes 16
  50.7 14.8 %copy-start.144 = (pred[4]{0:T(512)(128)(4,1)S(1)}, pred[4]{0:T(512)(128)(4,1)}, u32[]{:S(2)}) copy-start(pred[4]{0:T(512)(128)(4,1)} %get-tuple-element.315) | copy-start | bytes 16
  132.5 16.5 %collective-permute-start.3 = (bf16[1,4,64,512]{3,2,1,0:T(8,128)(2,1)}, bf16[1,4,64,512]{3,2,1,0:T(8,128)(2,1)S(1)}, u32[]{:S(2)}, u32[]{:S(2)}) collective-permute-start(bf16[1,4,64,512]{3,2,1,0:T(8,128)(2,1)} %get-tuple-element.287), channel_id=1, source_target_pairs={{8,0},{16,8},{24,16},{32,24},{40,32},{48,40},{56,48},{64,56},{72,6... | collective-permute-start | bytes 786440 | tf_op jit(solution)/shard_map/ppermute | solution.py:19
  137.1 11.0 %collective-permute-start.2 = (bf16[1,4,64,512]{3,2,1,0:T(8,128)(2,1)}, bf16[1,4,64,512]{3,2,1,0:T(8,128)(2,1)S(1)}, u32[]{:S(2)}, u32[]{:S(2)}) collective-permute-start(bf16[1,4,64,512]{3,2,1,0:T(8,128)(2,1)} %get-tuple-element.287), channel_id=1, source_target_pairs={{0,8},{8,16},{16,24},{24,32},{32,40},{40,48},{48,56},{56,64},{64,7... | collective-permute-start | bytes 786440 | tf_op jit(solution)/shard_map/ppermute | solution.py:18
  145.4 24.1 %copy-start.35 = (bf16[1,4,64,8,1,8]{2,5,4,3,1,0:T(8,128)(2,1)}, bf16[1,4,64,8,1,8]{2,5,4,3,1,0:T(8,128)(2,1)S(1)}, u32[]{:S(2)}) copy-start(bf16[1,4,64,8,1,8]{2,5,4,3,1,0:T(8,128)(2,1)S(1)} %fusion.35) | copy-start | bytes 98308
  149.3 14.1 %copy-start.185 = (pred[4]{0:T(512)(128)(4,1)S(1)}, pred[4]{0:T(512)(128)(4,1)}, u32[]{:S(2)}) copy-start(pred[4]{0:T(512)(128)(4,1)} %get-tuple-element.51) | copy-start | bytes 16
  149.3 14.1 %copy-start.221 = (pred[4]{0:T(512)(128)(4,1)S(1)}, pred[4]{0:T(512)(128)(4,1)}, u32[]{:S(2)}) copy-start(pred[4]{0:T(512)(128)(4,1)} %get-tuple-element.316) | copy-start | bytes 16
  149.4 14.8 %copy-start.181 = (pred[4]{0:T(512)(128)(4,1)S(1)}, pred[4]{0:T(512)(128)(4,1)}, u32[]{:S(2)}) copy-start(pred[4]{0:T(512)(128)(4,1)} %get-tuple-element.46) | copy-start | bytes 16
  149.4 14.8 %copy-start.217 = (pred[4]{0:T(512)(128)(4,1)S(1)}, pred[4]{0:T(512)(128)(4,1)}, u32[]{:S(2)}) copy-start(pred[4]{0:T(512)(128)(4,1)} %get-tuple-element.313) | copy-start | bytes 16
  233.6 15.8 %collective-permute-start.5 = (bf16[1,4,64,512]{3,2,1,0:T(8,128)(2,1)}, bf16[1,4,64,512]{3,2,1,0:T(8,128)(2,1)S(1)}, u32[]{:S(2)}, u32[]{:S(2)}) collective-permute-start(bf16[1,4,64,512]{3,2,1,0:T(8,128)(2,1)} %get-tuple-element.173), channel_id=1, source_target_pairs={{8,0},{16,8},{24,16},{32,24},{40,32},{48,40},{56,48},{64,56},{72,6... | collective-permute-start | bytes 786440 | tf_op jit(solution)/shard_map/ppermute | solution.py:19
  237.6 11.0 %collective-permute-start.4 = (bf16[1,4,64,512]{3,2,1,0:T(8,128)(2,1)}, bf16[1,4,64,512]{3,2,1,0:T(8,128)(2,1)S(1)}, u32[]{:S(2)}, u32[]{:S(2)}) collective-permute-start(bf16[1,4,64,512]{3,2,1,0:T(8,128)(2,1)} %get-tuple-element.173), channel_id=1, source_target_pairs={{0,8},{8,16},{16,24},{24,32},{32,40},{40,48},{48,56},{56,64},{64,7... | collective-permute-start | bytes 786440 | tf_op jit(solution)/shard_map/ppermute | solution.py:18
  245.8 24.1 %copy-start.36 = (bf16[1,4,64,8,1,8]{2,5,4,3,1,0:T(8,128)(2,1)}, bf16[1,4,64,8,1,8]{2,5,4,3,1,0:T(8,128)(2,1)S(1)}, u32[]{:S(2)}) copy-start(bf16[1,4,64,8,1,8]{2,5,4,3,1,0:T(8,128)(2,1)S(1)} %fusion.29) | copy-start | bytes 98308
  249.8 14.8 %copy-start.182 = (pred[4]{0:T(512)(128)(4,1)S(1)}, pred[4]{0:T(512)(128)(4,1)}, u32[]{:S(2)}) copy-start(pred[4]{0:T(512)(128)(4,1)} %get-tuple-element.46) | copy-start | bytes 16
  249.8 14.8 %copy-start.218 = (pred[4]{0:T(512)(128)(4,1)S(1)}, pred[4]{0:T(512)(128)(4,1)}, u32[]{:S(2)}) copy-start(pred[4]{0:T(512)(128)(4,1)} %get-tuple-element.313) | copy-start | bytes 16
  315.3 14.4 %copy-start.66 = (bf16[1,4,1,64,512]{4,3,1,2,0:T(8,128)(2,1)S(1)}, bf16[1,4,1,64,512]{4,3,1,2,0:T(8,128)(2,1)}, u32[]{:S(2)}) copy-start(bf16[1,4,1,64,512]{4,3,1,2,0:T(8,128)(2,1)} %copy.590) | copy-start | bytes 786436
  315.3 15.1 %copy-start.62 = (bf16[1,4,1,64,512]{4,3,1,2,0:T(8,128)(2,1)S(1)}, bf16[1,4,1,64,512]{4,3,1,2,0:T(8,128)(2,1)}, u32[]{:S(2)}) copy-start(bf16[1,4,1,64,512]{4,3,1,2,0:T(8,128)(2,1)} %copy.591) | copy-start | bytes 786436
  316.3 14.9 %copy-start.59 = (bf16[1,4,1,64,512]{4,3,1,2,0:T(8,128)(2,1)S(1)}, bf16[1,4,1,64,512]{4,3,1,2,0:T(8,128)(2,1)}, u32[]{:S(2)}) copy-start(bf16[1,4,1,64,512]{4,3,1,2,0:T(8,128)(2,1)} %copy.592) | copy-start | bytes 786436
  350.8 14.4 %copy-start.207 = (pred[4]{0:T(512)(128)(4,1)S(1)}, pred[4]{0:T(512)(128)(4,1)}, u32[]{:S(2)}) copy-start(pred[4]{0:T(512)(128)(4,1)} %copy-done.204) | copy-start | bytes 16
  350.8 14.4 %copy-start.251 = (pred[4]{0:T(512)(128)(4,1)S(1)}, pred[4]{0:T(512)(128)(4,1)}, u32[]{:S(2)}) copy-start(pred[4]{0:T(512)(128)(4,1)} %copy-done.248) | copy-start | bytes 16
  353.8 14.6 %copy-start.135 = (pred[4]{0:T(512)(128)(4,1)S(1)}, pred[4]{0:T(512)(128)(4,1)}, u32[]{:S(2)}) copy-start(pred[4]{0:T(512)(128)(4,1)} %copy-done.132) | copy-start | bytes 16
  353.8 14.6 %copy-start.155 = (pred[4]{0:T(512)(128)(4,1)S(1)}, pred[4]{0:T(512)(128)(4,1)}, u32[]{:S(2)}) copy-start(pred[4]{0:T(512)(128)(4,1)} %copy-done.152) | copy-start | bytes 16
  353.8 14.6 %copy-start.179 = (pred[4]{0:T(512)(128)(4,1)S(1)}, pred[4]{0:T(512)(128)(4,1)}, u32[]{:S(2)}) copy-start(pred[4]{0:T(512)(128)(4,1)} %copy-done.176) | copy-start | bytes 16
  353.8 14.6 %copy-start.331 = (pred[4]{0:T(512)(128)(4,1)S(1)}, pred[4]{0:T(512)(128)(4,1)}, u32[]{:S(2)}) copy-start(pred[4]{0:T(512)(128)(4,1)} %copy-done.328) | copy-start | bytes 16
  353.8 17.4 %collective-permute-start.7 = (bf16[1,4,64,512]{3,2,1,0:T(8,128)(2,1)S(1)}, bf16[1,4,64,512]{3,2,1,0:T(8,128)(2,1)S(1)}, u32[]{:S(2)}, u32[]{:S(2)}) collective-permute-start(bf16[1,4,64,512]{3,2,1,0:T(8,128)(2,1)S(1)} %get-tuple-element.289), channel_id=1, source_target_pairs={{8,0},{16,8},{24,16},{32,24},{40,32},{48,40},{56,48},{64,56},{72,6... | collective-permute-start | bytes 786440 | tf_op jit(solution)/shard_map/ppermute | solution.py:19
  357.7 12.6 %collective-permute-start.6 = (bf16[1,4,64,512]{3,2,1,0:T(8,128)(2,1)S(1)}, bf16[1,4,64,512]{3,2,1,0:T(8,128)(2,1)S(1)}, u32[]{:S(2)}, u32[]{:S(2)}) collective-permute-start(bf16[1,4,64,512]{3,2,1,0:T(8,128)(2,1)S(1)} %get-tuple-element.289), channel_id=1, source_target_pairs={{0,8},{8,16},{16,24},{24,32},{32,40},{40,48},{48,56},{56,64},{64,7... | collective-permute-start | bytes 786440 | tf_op jit(solution)/shard_map/ppermute | solution.py:18
  367.6 24.1 %copy-start.33 = (bf16[1,4,64,8,1,8]{2,5,4,3,1,0:T(8,128)(2,1)}, bf16[1,4,64,8,1,8]{2,5,4,3,1,0:T(8,128)(2,1)S(1)}, u32[]{:S(2)}) copy-start(bf16[1,4,64,8,1,8]{2,5,4,3,1,0:T(8,128)(2,1)S(1)} %fusion.23) | copy-start | bytes 98308
  370.2 255.3 %all-reduce.5.cloned.1.call-start = ((), (), s32[]{:S(2)}) async-start(), calls=%async_computation | async-start | bytes 3538944 | tf_op jit(solution)/shard_map/psum | solution.py:129
  371.6 14.8 %copy-start.183 = (pred[4]{0:T(512)(128)(4,1)S(1)}, pred[4]{0:T(512)(128)(4,1)}, u32[]{:S(2)}) copy-start(pred[4]{0:T(512)(128)(4,1)} %get-tuple-element.46) | copy-start | bytes 16
  371.6 14.8 %copy-start.219 = (pred[4]{0:T(512)(128)(4,1)S(1)}, pred[4]{0:T(512)(128)(4,1)}, u32[]{:S(2)}) copy-start(pred[4]{0:T(512)(128)(4,1)} %get-tuple-element.313) | copy-start | bytes 16
  437.4 16.2 %copy-start.67 = (bf16[1,4,1,64,512]{4,3,1,2,0:T(8,128)(2,1)S(1)}, bf16[1,4,1,64,512]{4,3,1,2,0:T(8,128)(2,1)}, u32[]{:S(2)}) copy-start(bf16[1,4,1,64,512]{4,3,1,2,0:T(8,128)(2,1)} %copy.662) | copy-start | bytes 786436
  437.4 16.9 %copy-start.63 = (bf16[1,4,1,64,512]{4,3,1,2,0:T(8,128)(2,1)S(1)}, bf16[1,4,1,64,512]{4,3,1,2,0:T(8,128)(2,1)}, u32[]{:S(2)}) copy-start(bf16[1,4,1,64,512]{4,3,1,2,0:T(8,128)(2,1)} %copy.663) | copy-start | bytes 786436
  439.1 15.9 %copy-start.44 = (bf16[1,4,1,64,512]{4,3,1,2,0:T(8,128)(2,1)S(1)}, bf16[1,4,1,64,512]{4,3,1,2,0:T(8,128)(2,1)}, u32[]{:S(2)}) copy-start(bf16[1,4,1,64,512]{4,3,1,2,0:T(8,128)(2,1)} %copy.664) | copy-start | bytes 786436
  440.8 14.9 %copy-start.10 = (bf16[1,4,64,512]{3,2,1,0:T(8,128)(2,1)S(1)}, bf16[1,4,64,512]{3,2,1,0:T(8,128)(2,1)}, u32[]{:S(2)}) copy-start(bf16[1,4,64,512]{3,2,1,0:T(8,128)(2,1)} %copy-done.9) | copy-start | bytes 786436
  (288 other events, 2517.8 us)
Sparse Core Ops, SparseCore 0:
  370.3 80.4 all-reduce.6
  463.2 162.1 all-reduce.4
